TPU v7x, 512 devices: a whole 4x4x16 slice. The times are simulated.
512 devices in a mesh: row: 32 (over z, core), col: 16 (over y, x).
Axes of the slice: x: 4, y: 4, z: 16, core: 2. Of those that a mesh axis runs over, the one named last changes fastest.
Arguments:
- weights: bfloat16 [2, 24576, 6144], P(None, 'row', 'col'), may hold values from -0.15625 to 0.15625
- pattern: int32 [2, 192, 48], P(None, 'row', 'col'), may hold values 0 or 1
- sketch: bfloat16 [6144, 512], P('col'), may hold values from -6 to 6
Outputs:
- basis: float32 [2, 24576, 512], P(None, ('row', 'col'))
Inputs may be any that keep to these rules, and one draw needn't show every extreme that they name: `pattern`: 1 marks a block of the sparse part, 0 a block of the residual.
All inputs are finite; a program needn't handle non-finite values.
Results may differ from a plain program's by a relative error of at most 0.0003.
Values sent between devices are 32-bit elements; how exact they have to be, the bound alone decides.
No kernel may reach another device: no remote copies, remote signals or barrier semaphores. Data moves between devices by JAX's collectives and lax.ppermute only.
A program may use at most 64 MiB of HBM per device.

v0:
```python
import jax
import jax.numpy as jnp
from jax import lax
from jax.sharding import PartitionSpec as P

M = 24576
BLOCK = 128
LAYERS = 2


def make_basis(rows_here, gram):
    lower = jnp.linalg.cholesky(gram)
    solved = lax.linalg.triangular_solve(
        lower, rows_here, left_side=False, lower=True, transpose_a=True
    )
    return solved * jnp.sqrt(jnp.float32(M))


def local_gram(rows_here):
    return lax.dot_general(
        rows_here,
        rows_here,
        (((0,), (0,)), ((), ())),
        precision=lax.Precision.HIGHEST,
        preferred_element_type=jnp.float32,
    )


def body(weights, pattern, sketch):
    row_count = weights.shape[1]
    col_count = weights.shape[2]
    outputs = []
    for layer in range(LAYERS):
        keep = (1 - pattern[layer]).astype(jnp.bfloat16)
        shaped = (
            weights[layer].reshape(row_count // BLOCK, BLOCK, col_count // BLOCK, BLOCK)
            * keep[:, None, :, None]
        )
        leftover = shaped.reshape(row_count, col_count)
        rows_here = lax.psum_scatter(
            jnp.dot(leftover, sketch, preferred_element_type=jnp.float32),
            "col",
            scatter_dimension=0,
            tiled=True,
        )
        sampled = lax.all_gather(rows_here, "col", axis=0, tiled=True)
        gram = lax.psum(local_gram(sampled), "row") / M
        outputs.append(make_basis(rows_here, gram))
    return jnp.stack(outputs, axis=0)


def solution(mesh):
    return jax.shard_map(
        body,
        mesh=mesh,
        in_specs=(P(None, "row", "col"), P(None, "row", "col"), P("col", None)),
        out_specs=P(None, ("row", "col"), None),
        check_vma=False,
    )
```

profile of v0, /device:TPU:1, one launch (start us, length us, event | category | flops | bytes accessed | tf_op | source)
XLA Modules:
  0.0 823.3 jit_solution(7290686633852218556)
XLA Ops:
  6.5 0.8 subtract_convert_fusion.1
  7.3 1.4 fusion.70
  9.1 1.8 fusion.4
  11.4 1.8 fusion.2
  13.3 91.7 %reduce-scatter.3.cloned.1.call-done = f32[48,512]{1,0:T(8,128)} async-done(((f32[768,512]{1,0:T(8,128)}), f32[48,512]{1,0:T(8,128)}) %reduce-scatter.3.cloned.1.call-update) | async-done | bytes 98320 | tf_op jit(solution)/shard_map/reduce_scatter | solution.py:40
  105.0 93.3 %reduce-scatter.5.cloned.1.call-done = f32[48,512]{1,0:T(8,128)} async-done(((f32[768,512]{1,0:T(8,128)}), f32[48,512]{1,0:T(8,128)}) %reduce-scatter.5.cloned.1.call-update) | async-done | bytes 98320 | tf_op jit(solution)/shard_map/reduce_scatter | solution.py:40
  198.4 61.8 %all-gather.3.cloned.1.call-done = f32[768,512]{1,0:T(8,128)} async-done(((f32[48,512]{1,0:T(8,128)}), f32[768,512]{1,0:T(8,128)}) %all-gather.3.cloned.1.call-update) | async-done | bytes 1572880 | tf_op jit(solution)/shard_map/all_gather | solution.py:46
  260.2 5.6 fusion.71
  265.8 55.8 %all-gather.5.cloned.1.call-done = f32[768,512]{1,0:T(8,128)} async-done(((f32[48,512]{1,0:T(8,128)}), f32[768,512]{1,0:T(8,128)}) %all-gather.5.cloned.1.call-update) | async-done | bytes 1572880 | tf_op jit(solution)/shard_map/all_gather | solution.py:46
  321.6 5.6 fusion.72
  327.2 217.0 %all-reduce.4.cloned.1.call-done = (f32[512,512]{0,1:T(8,128)}, f32[512,512]{0,1:T(8,128)}) async-done(((f32[512,512]{0,1:T(8,128)}, f32[512,512]{0,1:T(8,128)}), (f32[512,512]{0,1:T(8,128)}, f32[512,512]{0,1:T(8,128)})) %all-reduce.4.cloned.1.call-update) | async-done | bytes 2097168 | tf_op jit(solution)/shard_map/psum | solution.py:47
  544.2 1.3 broadcast_multiply_fusion.1
  545.9 0.9 copy-done.2
  547.1 11.7 %cholesky.286 = f32[128,128]{1,0:T(8,128)S(1)} custom-call(f32[128,128]{1,0:T(8,128)S(1)} %cholesky.426), custom_call_target="Cholesky" | custom-call | tf_op jit(solution)/shard_map/jit(cholesky)/cholesky | solution.py:12
  558.8 10.0 %custom-call.27 = f32[1,128,128]{1,2,0:T(8,128)S(1)} custom-call(f32[1,128,128]{2,1,0:T(8,128)S(1)} %get-tuple-element.56), custom_call_target="InvertDiagBlocksLowerTriangular" | custom-call | tf_op jit(solution)/shard_map/jit(cholesky)/cholesky | solution.py:12
  569.6 11.7 %cholesky.305 = f32[128,128]{1,0:T(8,128)S(1)} custom-call(f32[128,128]{1,0:T(8,128)S(1)} %cholesky.430), custom_call_target="Cholesky" | custom-call | tf_op jit(solution)/shard_map/jit(cholesky)/cholesky | solution.py:12
  581.4 0.6 compare_reduce_fusion.6
  582.0 0.7 compare_reduce_fusion.7
  582.7 9.8 %custom-call.28 = f32[1,128,128]{1,2,0:T(8,128)S(1)} custom-call(f32[1,128,128]{2,1,0:T(8,128)S(1)} %get-tuple-element.53), custom_call_target="InvertDiagBlocksLowerTriangular" | custom-call | tf_op jit(solution)/shard_map/jit(cholesky)/cholesky | solution.py:12
  593.2 11.7 %cholesky.326 = f32[128,128]{1,0:T(8,128)S(1)} custom-call(f32[128,128]{1,0:T(8,128)S(1)} %cholesky.435), custom_call_target="Cholesky" | custom-call | tf_op jit(solution)/shard_map/jit(cholesky)/cholesky | solution.py:12
  605.0 0.7 compare_reduce_fusion.5
  605.6 10.2 %custom-call.29 = f32[1,128,128]{1,2,0:T(8,128)S(1)} custom-call(f32[1,128,128]{2,1,0:T(8,128)S(1)} %get-tuple-element.50), custom_call_target="InvertDiagBlocksLowerTriangular" | custom-call | tf_op jit(solution)/shard_map/jit(cholesky)/cholesky | solution.py:12
  616.4 11.7 %cholesky.343 = f32[128,128]{1,0:T(8,128)S(1)} custom-call(f32[128,128]{1,0:T(8,128)S(1)} %convolution_subtract_fusion.5), custom_call_target="Cholesky" | custom-call | tf_op jit(solution)/shard_map/jit(cholesky)/cholesky | solution.py:12
  628.2 0.7 compare_reduce_fusion.4
  631.6 8.1 while.4
  632.3 1.3 bitcast_dynamic-update-slice_fusion.4
  634.3 1.3 bitcast_dynamic-update-slice_fusion.4
  636.3 1.3 bitcast_dynamic-update-slice_fusion.4
  638.4 1.3 bitcast_dynamic-update-slice_fusion.4
  639.7 39.5 %custom-call.30 = f32[4,128,128]{1,2,0:T(8,128)S(1)} custom-call(f32[4,128,128]{2,1,0:T(8,128)S(1)} %get-tuple-element.21), custom_call_target="InvertDiagBlocksLowerTriangular" | custom-call | tf_op jit(solution)/shard_map/triangular_solve/custom-call.3 | solution.py:13
  680.8 0.7 fusion.24
  682.2 11.7 %cholesky.358 = f32[128,128]{1,0:T(8,128)S(1)} custom-call(f32[128,128]{1,0:T(8,128)S(1)} %cholesky.439), custom_call_target="Cholesky" | custom-call | tf_op jit(solution)/shard_map/jit(cholesky)/cholesky | solution.py:12
  693.9 9.8 %custom-call.31 = f32[1,128,128]{1,2,0:T(8,128)S(1)} custom-call(f32[1,128,128]{2,1,0:T(8,128)S(1)} %get-tuple-element.66), custom_call_target="InvertDiagBlocksLowerTriangular" | custom-call | tf_op jit(solution)/shard_map/jit(cholesky)/cholesky | solution.py:12
  704.5 11.7 %cholesky.377 = f32[128,128]{1,0:T(8,128)S(1)} custom-call(f32[128,128]{1,0:T(8,128)S(1)} %cholesky.443), custom_call_target="Cholesky" | custom-call | tf_op jit(solution)/shard_map/jit(cholesky)/cholesky | solution.py:12
  716.9 0.7 compare_reduce_fusion.3
  717.6 10.0 %custom-call.32 = f32[1,128,128]{1,2,0:T(8,128)S(1)} custom-call(f32[1,128,128]{2,1,0:T(8,128)S(1)} %get-tuple-element.63), custom_call_target="InvertDiagBlocksLowerTriangular" | custom-call | tf_op jit(solution)/shard_map/jit(cholesky)/cholesky | solution.py:12
  728.3 11.7 %cholesky.398 = f32[128,128]{1,0:T(8,128)S(1)} custom-call(f32[128,128]{1,0:T(8,128)S(1)} %cholesky.448), custom_call_target="Cholesky" | custom-call | tf_op jit(solution)/shard_map/jit(cholesky)/cholesky | solution.py:12
  740.1 0.7 compare_reduce_fusion.1
  740.7 9.8 %custom-call.33 = f32[1,128,128]{1,2,0:T(8,128)S(1)} custom-call(f32[1,128,128]{2,1,0:T(8,128)S(1)} %get-tuple-element.60), custom_call_target="InvertDiagBlocksLowerTriangular" | custom-call | tf_op jit(solution)/shard_map/jit(cholesky)/cholesky | solution.py:12
  751.1 12.0 %cholesky.415 = f32[128,128]{1,0:T(8,128)S(1)} custom-call(f32[128,128]{1,0:T(8,128)S(1)} %convolution_subtract_fusion.4), custom_call_target="Cholesky" | custom-call | tf_op jit(solution)/shard_map/jit(cholesky)/cholesky | solution.py:12
  763.1 0.7 compare_reduce_fusion
  766.5 8.1 while.5
  767.2 1.3 bitcast_dynamic-update-slice_fusion.5
  769.3 1.3 bitcast_dynamic-update-slice_fusion.5
  771.3 1.3 bitcast_dynamic-update-slice_fusion.5
  773.3 1.3 bitcast_dynamic-update-slice_fusion.5
  774.7 39.3 %custom-call.34 = f32[4,128,128]{1,2,0:T(8,128)S(1)} custom-call(f32[4,128,128]{2,1,0:T(8,128)S(1)} %get-tuple-element.22), custom_call_target="InvertDiagBlocksLowerTriangular" | custom-call | tf_op jit(solution)/shard_map/triangular_solve/custom-call.3 | solution.py:13
  815.6 0.7 pad_maximum_fusion
  (97 shorter events, 16.1 us)
Async XLA Ops:
  6.5 2.6 copy-start
  6.5 98.4 %reduce-scatter.3.cloned.1.call-start = ((), (), s32[]{:S(2)}) async-start(), calls=%async_computation.2 | async-start | bytes 1671168 | tf_op jit(solution)/shard_map/reduce_scatter | solution.py:40
  10.9 187.4 %reduce-scatter.5.cloned.1.call-start = ((), (), s32[]{:S(2)}) async-start(), calls=%async_computation.4 | async-start | bytes 1671168 | tf_op jit(solution)/shard_map/reduce_scatter | solution.py:40
  13.2 247.0 %all-gather.3.cloned.1.call-start = ((), (), s32[]{:S(2)}) async-start(), calls=%async_computation.3 | async-start | bytes 1671168 | tf_op jit(solution)/shard_map/all_gather | solution.py:46
  104.9 216.6 %all-gather.5.cloned.1.call-start = ((), (), s32[]{:S(2)}) async-start(), calls=%async_computation.5 | async-start | bytes 1671168 | tf_op jit(solution)/shard_map/all_gather | solution.py:46
  198.4 345.9 %all-reduce.4.cloned.1.call-start = ((), (), s32[]{:S(2)}) async-start(), calls=%async_computation.6 | async-start | bytes 4194304 | tf_op jit(solution)/shard_map/psum | solution.py:47
  545.6 1.2 copy-start.2
  631.4 47.8 %copy-start.4 = (f32[48,512]{1,0:T(8,128)S(1)}, f32[48,512]{1,0:T(8,128)}, u32[]{:S(2)}) copy-start(f32[48,512]{1,0:T(8,128)} %reduce-scatter.3.cloned.1.call-done) | copy-start | bytes 294916
  631.5 49.9 %copy-start.1 = (f32[512,512]{0,1:T(8,128)S(1)}, f32[512,512]{0,1:T(8,128)}, u32[]{:S(2)}) copy-start(f32[512,512]{0,1:T(8,128)} %get-tuple-element.39) | copy-start | bytes 3145732
  766.4 47.7 %copy-start.3 = (f32[48,512]{1,0:T(8,128)S(1)}, f32[48,512]{1,0:T(8,128)}, u32[]{:S(2)}) copy-start(f32[48,512]{1,0:T(8,128)} %reduce-scatter.5.cloned.1.call-done) | copy-start | bytes 294916
  766.5 49.1 %copy-start.5 = (f32[1,48,512]{2,1,0:T(8,128)S(1)}, f32[1,48,512]{2,1,0:T(8,128)}, u32[]{:S(2)}) copy-start(f32[1,48,512]{2,1,0:T(8,128)} %fusion.24) | copy-start | bytes 294916
Sparse Core Ops, SparseCore 0:
  11.4 93.4 reduce-scatter.2
  109.0 89.2 reduce-scatter.4
  201.4 58.8 all-gather.2
  263.1 58.4 all-gather.4
  327.3 216.8 all-reduce.3
where the time goes:
time: 833 us; the launch traced here: 823 us
  waiting for transfers between devices  520 us (62%)
  other arithmetic  242 us (29%)
  matrix products  21.5 us (3%)
  local copies, waits for them, and re-layouts  20.2 us (2%)
  between operations  19.1 us (2%)
    psum x1, waiting for transfers between devices, body(): gram = lax.psum(local_gram(sampled), 'row') / M  217 us
    reduce_scatter x2, waiting for transfers between devices, body(): lax.psum_scatter(jnp.dot(leftover, sketch, preferred_element_type=jnp.flo...  185 us
    another operation x30, other arithmetic, make_basis(): lower = jnp.linalg.cholesky(gram)  159 us
    all_gather x2, waiting for transfers between devices, body(): sampled = lax.all_gather(rows_here, 'col', axis=0, tiled=True)  118 us
    another operation x5, other arithmetic, make_basis(): lax.linalg.triangular_solve(lower, rows_here, left_side=False, lower=True...  79.1 us
  transfers between devices with their start and end apart: 5, of which 5 were waited for; matrix products, arithmetic and copies ran while one was open for 1% of the time, Pallas kernels for 0%

commit v1 on v0

--- a/solution.py
+++ b/solution.py
@@ -43,7 +43,10 @@
             scatter_dimension=0,
             tiled=True,
         )
-        sampled = lax.all_gather(rows_here, "col", axis=0, tiled=True)
+        size = lax.axis_size("col")
+        blocks = jnp.stack([rows_here for _ in range(size)])
+        blocks = lax.all_to_all(blocks, "col", split_axis=0, concat_axis=0)
+        sampled = jnp.concatenate(blocks, axis=0)
         gram = lax.psum(local_gram(sampled), "row") / M
         outputs.append(make_basis(rows_here, gram))
     return jnp.stack(outputs, axis=0)

time: 833 us -> 730 us (0.88)
  waiting for transfers between devices: 520 us -> 414 us
  starting transfers between devices: 0.16 us -> 9.03 us
    all_gather x2 -> x0, waiting for transfers between devices: 118 us -> none  [body(): sampled = lax.all_gather(rows_here, 'col', axis=0, tiled=True)]
    all_to_all x0 -> x2, waiting for transfers between devices: none -> 15.9 us  [body(): blocks = lax.all_to_all(blocks, 'col', split_axis=0, concat_axis=0)]
    all_to_all x0 -> x2, starting transfers between devices: none -> 8.77 us  [body(): blocks = lax.all_to_all(blocks, 'col', split_axis=0, concat_axis=0)]
  transfers between devices with their start and end apart: 5 -> 5, of which waited for: 5 -> 4; matrix products, arithmetic and copies ran while one was open for 1% -> 1% of each run, Pallas kernels for 0% -> 0%
where the time goes in v1:
time: 730 us; the launch traced here: 727 us
  waiting for transfers between devices  414 us (57%)
  other arithmetic  242 us (33%)
  local copies, waits for them, and re-layouts  24.7 us (3%)
  between operations  19 us (3%)
  matrix products  17.8 us (2%)
  starting transfers between devices  9.03 us (1%)
    psum x1, waiting for transfers between devices, body(): gram = lax.psum(local_gram(sampled), 'row') / M  218 us
    reduce_scatter x2, waiting for transfers between devices, body(): lax.psum_scatter(jnp.dot(leftover, sketch, preferred_element_type=jnp.flo...  180 us
    another operation x30, other arithmetic, make_basis(): lower = jnp.linalg.cholesky(gram)  159 us
    another operation x5, other arithmetic, make_basis(): lax.linalg.triangular_solve(lower, rows_here, left_side=False, lower=True...  79.1 us
    another operation x27, local copies, waits for them, and re-layouts, make_basis(): lax.linalg.triangular_solve(lower, rows_here, left_side=False, lower=True...  16.2 us
    all_to_all x2, waiting for transfers between devices, body(): blocks = lax.all_to_all(blocks, 'col', split_axis=0, concat_axis=0)  15.9 us
  transfers between devices with their start and end apart: 5, of which 4 were waited for; matrix products, arithmetic and copies ran while one was open for 1% of the time, Pallas kernels for 0%

profile of v1, /device:TPU:1, one launch (start us, length us, event | category | flops | bytes accessed | tf_op | source)
XLA Modules:
  0.0 727.3 jit_solution(9606499625010721038)
XLA Ops:
  6.5 0.8 subtract_convert_fusion.1
  7.3 1.4 fusion.70
  9.1 1.8 fusion.2
  11.4 1.8 fusion.4
  13.2 91.7 %reduce-scatter.5.cloned.1.call-done = f32[48,512]{1,0:T(8,128)} async-done(((f32[768,512]{1,0:T(8,128)}), f32[48,512]{1,0:T(8,128)}) %reduce-scatter.5.cloned.1.call-update) | async-done | bytes 98320 | tf_op jit(solution)/shard_map/reduce_scatter | solution.py:40
  105.0 2.3 stack.12
  107.2 4.4 all-to-all-start.1
  111.6 88.6 %reduce-scatter.3.cloned.1.call-done = f32[48,512]{1,0:T(8,128)} async-done(((f32[768,512]{1,0:T(8,128)}), f32[48,512]{1,0:T(8,128)}) %reduce-scatter.3.cloned.1.call-update) | async-done | bytes 98320 | tf_op jit(solution)/shard_map/reduce_scatter | solution.py:40
  200.2 2.2 stack.10
  202.4 4.4 all-to-all-start
  207.0 3.7 convolution_bitcast_fusion
  210.8 15.9 %all-to-all-done = f32[16,48,512]{2,1,0:T(8,128)S(1)} async-done(((f32[16,48,512]{2,1,0:T(8,128)}), f32[16,48,512]{2,1,0:T(8,128)S(1)}, u32[]{:S(2)}, u32[]{:S(2)}) %all-to-all-start) | async-done | bytes 1572896 | tf_op jit(solution)/shard_map/all_to_all | solution.py:48
  226.7 3.7 convolution_bitcast_fusion.1
  230.4 217.9 %all-reduce.4.cloned.1.call-done = (f32[512,512]{0,1:T(8,128)}, f32[512,512]{0,1:T(8,128)}) async-done(((f32[512,512]{0,1:T(8,128)}, f32[512,512]{0,1:T(8,128)}), (f32[512,512]{0,1:T(8,128)}, f32[512,512]{0,1:T(8,128)})) %all-reduce.4.cloned.1.call-update) | async-done | bytes 2097168 | tf_op jit(solution)/shard_map/psum | solution.py:50
  448.3 1.3 broadcast_multiply_fusion.1
  449.9 0.9 copy-done.2
  451.1 11.7 %cholesky.286 = f32[128,128]{1,0:T(8,128)S(1)} custom-call(f32[128,128]{1,0:T(8,128)S(1)} %cholesky.426), custom_call_target="Cholesky" | custom-call | tf_op jit(solution)/shard_map/jit(cholesky)/cholesky | solution.py:12
  462.8 10.0 %custom-call.27 = f32[1,128,128]{1,2,0:T(8,128)S(1)} custom-call(f32[1,128,128]{2,1,0:T(8,128)S(1)} %get-tuple-element.56), custom_call_target="InvertDiagBlocksLowerTriangular" | custom-call | tf_op jit(solution)/shard_map/jit(cholesky)/cholesky | solution.py:12
  473.6 11.7 %cholesky.305 = f32[128,128]{1,0:T(8,128)S(1)} custom-call(f32[128,128]{1,0:T(8,128)S(1)} %cholesky.430), custom_call_target="Cholesky" | custom-call | tf_op jit(solution)/shard_map/jit(cholesky)/cholesky | solution.py:12
  486.0 0.7 compare_reduce_fusion.7
  486.7 9.8 %custom-call.28 = f32[1,128,128]{1,2,0:T(8,128)S(1)} custom-call(f32[1,128,128]{2,1,0:T(8,128)S(1)} %get-tuple-element.53), custom_call_target="InvertDiagBlocksLowerTriangular" | custom-call | tf_op jit(solution)/shard_map/jit(cholesky)/cholesky | solution.py:12
  497.2 11.7 %cholesky.326 = f32[128,128]{1,0:T(8,128)S(1)} custom-call(f32[128,128]{1,0:T(8,128)S(1)} %cholesky.435), custom_call_target="Cholesky" | custom-call | tf_op jit(solution)/shard_map/jit(cholesky)/cholesky | solution.py:12
  508.9 0.7 compare_reduce_fusion.5
  509.7 10.2 %custom-call.29 = f32[1,128,128]{1,2,0:T(8,128)S(1)} custom-call(f32[1,128,128]{2,1,0:T(8,128)S(1)} %get-tuple-element.50), custom_call_target="InvertDiagBlocksLowerTriangular" | custom-call | tf_op jit(solution)/shard_map/jit(cholesky)/cholesky | solution.py:12
  520.5 11.7 %cholesky.343 = f32[128,128]{1,0:T(8,128)S(1)} custom-call(f32[128,128]{1,0:T(8,128)S(1)} %convolution_subtract_fusion.5), custom_call_target="Cholesky" | custom-call | tf_op jit(solution)/shard_map/jit(cholesky)/cholesky | solution.py:12
  535.6 8.2 %while.4 = (s32[]{:T(128)}, f32[512,512]{1,0:T(8,128)S(1)}, s32[4,2]{0,1:T(2,128)S(1)}, f32[4,128,128]{2,1,0:T(8,128)S(1)}, s32[]{:T(128)}) while((s32[]{:T(128)}, f32[512,512]{1,0:T(8,128)S(1)}, s32[4,2]{0,1:T(2,128)S(1)}, f32[4,128,128]{2,1,0:T(8,128)S(1)}, s32[]{:T(128)}) %tuple.56), condition=%wide.while_cond, body=%wide.while_body.sunk | while | flops 2 | bytes 131181 | solution.py:13
  536.3 1.3 bitcast_dynamic-update-slice_fusion.4
  538.4 1.3 bitcast_dynamic-update-slice_fusion.4
  540.4 1.3 bitcast_dynamic-update-slice_fusion.4
  542.4 1.3 bitcast_dynamic-update-slice_fusion.4
  543.8 39.5 %custom-call.30 = f32[4,128,128]{1,2,0:T(8,128)S(1)} custom-call(f32[4,128,128]{2,1,0:T(8,128)S(1)} %get-tuple-element.21), custom_call_target="InvertDiagBlocksLowerTriangular" | custom-call | tf_op jit(solution)/shard_map/triangular_solve/custom-call.3 | solution.py:13
  586.3 11.7 %cholesky.358 = f32[128,128]{1,0:T(8,128)S(1)} custom-call(f32[128,128]{1,0:T(8,128)S(1)} %cholesky.439), custom_call_target="Cholesky" | custom-call | tf_op jit(solution)/shard_map/jit(cholesky)/cholesky | solution.py:12
  598.0 9.8 %custom-call.31 = f32[1,128,128]{1,2,0:T(8,128)S(1)} custom-call(f32[1,128,128]{2,1,0:T(8,128)S(1)} %get-tuple-element.66), custom_call_target="InvertDiagBlocksLowerTriangular" | custom-call | tf_op jit(solution)/shard_map/jit(cholesky)/cholesky | solution.py:12
  608.6 11.7 %cholesky.377 = f32[128,128]{1,0:T(8,128)S(1)} custom-call(f32[128,128]{1,0:T(8,128)S(1)} %cholesky.443), custom_call_target="Cholesky" | custom-call | tf_op jit(solution)/shard_map/jit(cholesky)/cholesky | solution.py:12
  621.0 0.7 compare_reduce_fusion.3
  621.7 10.0 %custom-call.32 = f32[1,128,128]{1,2,0:T(8,128)S(1)} custom-call(f32[1,128,128]{2,1,0:T(8,128)S(1)} %get-tuple-element.63), custom_call_target="InvertDiagBlocksLowerTriangular" | custom-call | tf_op jit(solution)/shard_map/jit(cholesky)/cholesky | solution.py:12
  632.4 11.7 %cholesky.398 = f32[128,128]{1,0:T(8,128)S(1)} custom-call(f32[128,128]{1,0:T(8,128)S(1)} %cholesky.448), custom_call_target="Cholesky" | custom-call | tf_op jit(solution)/shard_map/jit(cholesky)/cholesky | solution.py:12
  644.1 0.7 compare_reduce_fusion.1
  644.9 9.8 %custom-call.33 = f32[1,128,128]{1,2,0:T(8,128)S(1)} custom-call(f32[1,128,128]{2,1,0:T(8,128)S(1)} %get-tuple-element.60), custom_call_target="InvertDiagBlocksLowerTriangular" | custom-call | tf_op jit(solution)/shard_map/jit(cholesky)/cholesky | solution.py:12
  655.3 12.0 %cholesky.415 = f32[128,128]{1,0:T(8,128)S(1)} custom-call(f32[128,128]{1,0:T(8,128)S(1)} %convolution_subtract_fusion.4), custom_call_target="Cholesky" | custom-call | tf_op jit(solution)/shard_map/jit(cholesky)/cholesky | solution.py:12
  667.3 0.7 compare_reduce_fusion
  670.7 8.1 %while.5 = (s32[]{:T(128)}, f32[512,512]{1,0:T(8,128)S(1)}, s32[4,2]{0,1:T(2,128)S(1)}, f32[4,128,128]{2,1,0:T(8,128)S(1)}, s32[]{:T(128)}) while((s32[]{:T(128)}, f32[512,512]{1,0:T(8,128)S(1)}, s32[4,2]{0,1:T(2,128)S(1)}, f32[4,128,128]{2,1,0:T(8,128)S(1)}, s32[]{:T(128)}) %tuple.66), condition=%wide.while_cond.clone, body=%wide.while_body.clone.sunk | while | flops 2 | bytes 131181 | solution.py:13
  671.4 1.3 bitcast_dynamic-update-slice_fusion.5
  673.4 1.3 bitcast_dynamic-update-slice_fusion.5
  675.5 1.3 bitcast_dynamic-update-slice_fusion.5
  677.5 1.3 bitcast_dynamic-update-slice_fusion.5
  678.9 39.3 %custom-call.34 = f32[4,128,128]{1,2,0:T(8,128)S(1)} custom-call(f32[4,128,128]{2,1,0:T(8,128)S(1)} %get-tuple-element.22), custom_call_target="InvertDiagBlocksLowerTriangular" | custom-call | tf_op jit(solution)/shard_map/triangular_solve/custom-call.3 | solution.py:13
  719.8 0.7 pad_maximum_fusion
  (97 shorter events, 18.1 us)
Async XLA Ops:
  6.5 2.6 copy-start
  6.5 98.4 %reduce-scatter.5.cloned.1.call-start = ((), (), s32[]{:S(2)}) async-start(), calls=%async_computation.5 | async-start | bytes 1671168 | tf_op jit(solution)/shard_map/reduce_scatter | solution.py:40
  10.9 189.2 %reduce-scatter.3.cloned.1.call-start = ((), (), s32[]{:S(2)}) async-start(), calls=%async_computation.4 | async-start | bytes 1671168 | tf_op jit(solution)/shard_map/reduce_scatter | solution.py:40
  107.2 93.0 %all-to-all-start.1 = ((f32[16,48,512]{2,1,0:T(8,128)}), f32[16,48,512]{2,1,0:T(8,128)S(1)}, u32[]{:S(2)}, u32[]{:S(2)}) async-start(f32[16,48,512]{2,1,0:T(8,128)} %stack.12), calls=%async_computation.3 | async-start | bytes 3145728 | tf_op jit(solution)/shard_map/all_to_all | solution.py:48
  202.4 24.2 %all-to-all-start = ((f32[16,48,512]{2,1,0:T(8,128)}), f32[16,48,512]{2,1,0:T(8,128)S(1)}, u32[]{:S(2)}, u32[]{:S(2)}) async-start(f32[16,48,512]{2,1,0:T(8,128)} %stack.10), calls=%async_computation.1 | async-start | bytes 3145728 | tf_op jit(solution)/shard_map/all_to_all | solution.py:48
  206.8 241.4 %all-reduce.4.cloned.1.call-start = ((), (), s32[]{:S(2)}) async-start(), calls=%async_computation.6 | async-start | bytes 4194304 | tf_op jit(solution)/shard_map/psum | solution.py:50
  449.6 1.2 copy-start.2
  535.5 47.9 %copy-start.4 = (f32[48,512]{1,0:T(8,128)S(1)}, f32[48,512]{1,0:T(8,128)}, u32[]{:S(2)}) copy-start(f32[48,512]{1,0:T(8,128)} %reduce-scatter.3.cloned.1.call-done) | copy-start | bytes 294916
  535.6 49.9 %copy-start.1 = (f32[512,512]{0,1:T(8,128)S(1)}, f32[512,512]{0,1:T(8,128)}, u32[]{:S(2)}) copy-start(f32[512,512]{0,1:T(8,128)} %get-tuple-element.39) | copy-start | bytes 3145732
  670.5 47.7 %copy-start.3 = (f32[48,512]{1,0:T(8,128)S(1)}, f32[48,512]{1,0:T(8,128)}, u32[]{:S(2)}) copy-start(f32[48,512]{1,0:T(8,128)} %reduce-scatter.5.cloned.1.call-done) | copy-start | bytes 294916
  670.7 49.1 %copy-start.5 = (f32[1,48,512]{2,1,0:T(8,128)S(1)}, f32[1,48,512]{2,1,0:T(8,128)}, u32[]{:S(2)}) copy-start(f32[1,48,512]{2,1,0:T(8,128)} %fusion.24) | copy-start | bytes 294916
Sparse Core Ops, SparseCore 0:
  11.4 93.4 reduce-scatter.4
  109.0 91.1 reduce-scatter.2
  230.5 217.7 all-reduce.3
